TPU v7x, 32 devices: a whole 2x2x4 slice. The times are simulated.
32 devices in a mesh: query: 8 (over z, y), store: 4 (over x, core).
Axes of the slice: x: 2, y: 2, z: 4, core: 2. Of those that a mesh axis runs over, the one named last changes fastest.
Arguments:
- in_rows: bfloat16 [8, 16384, 64], P('query', 'store'), may hold values from -6 to 6
- out_rows: bfloat16 [8, 16384, 128], P('query', 'store'), may hold values from -0.625 to 0.625
- row_doc: int32 [8, 16384], P('query', 'store'), may hold values from 0 to 31
- row_pos: int32 [8, 16384], P('query', 'store'), may hold values from 0 to 255
- doc_len: int32 [8, 128], P('query', 'store'), may hold values from 128 to 256
- eig_in: float32 [64], replicated, may hold values from 0.25 to 2
- eig_out: float32 [128], replicated, may hold values from 0.25 to 2
- basis_in: float32 [64, 64], replicated, may hold values from -0.75 to 0.75
- basis_out: float32 [128, 128], replicated, may hold values from -0.5 to 0.5
- train_feats: bfloat16 [8, 768, 8192], P('query', 'store'), may hold values from -0.0625 to 0.0625
Outputs:
- scores: bfloat16 [8, 128, 768], P('query', None, 'store')
Inputs may be any that keep to these rules, and one draw needn't show every extreme that they name: On each device the 4096 rows form 8 blocks of 512 rows in order; the rows of block j belong to documents of group j in the same store column, and row_doc names the document among that destination's 32.
All inputs are finite; a program needn't handle non-finite values.
Results may differ from a plain program's by a relative error of at most 0.0049.
Values may be sent and summed in bfloat16 or wider, within the bound.
A program may use at most 64 MiB of HBM per device.

v0:
```python
import math
import jax
import jax.numpy as jnp
from jax import lax
from jax.sharding import PartitionSpec as P

damping = 0.1
highest = lax.Precision.HIGHEST


def from_behind(x, axis, by):
    devices = lax.axis_size(axis)
    return lax.ppermute(x, axis, [(i, (i + by) % devices) for i in range(devices)])


def precondition(gradients, scaling, basis_in, basis_out):
    in_width = basis_in.shape[0]
    out_width = basis_out.shape[0]
    doc_count = gradients.shape[1] // in_width
    rotated = jnp.dot(basis_out.T, gradients, precision=highest)
    turned = jnp.dot(rotated.reshape(out_width * doc_count, in_width), basis_in, precision=highest)
    turned = turned.reshape(out_width, doc_count, in_width) * scaling[:, None, :]
    restored = jnp.dot(
        basis_out, turned.reshape(out_width, doc_count * in_width), precision=highest
    )
    final_map = jnp.dot(
        restored.reshape(out_width * doc_count, in_width), basis_in.T, precision=highest
    )
    final_map = final_map.reshape(out_width, doc_count, in_width)
    return (
        jnp.transpose(final_map, (1, 0, 2))
        .reshape(doc_count, out_width * in_width)
        .astype(jnp.bfloat16)
    )


def record(score_table, query_block, anchor, train_slab):
    partial_scores = lax.dot_general(
        query_block, train_slab, (((1,), (1,)), ((), ())), preferred_element_type=jnp.float32
    )
    return lax.dynamic_update_slice_in_dim(
        score_table, partial_scores.astype(jnp.bfloat16), anchor * query_block.shape[0], 0
    )


def on_device(
    in_rows, out_rows, row_doc, row_pos, doc_len, eig_in, eig_out, basis_in, basis_out, train_feats
):
    doc_count = doc_len.shape[1]
    in_width = in_rows.shape[2]
    packed_keys = row_doc * 65536 + row_pos
    inputs_side, grads_side, keys_side = (
        lax.all_to_all(in_rows, "query", split_axis=1, concat_axis=1, tiled=True),
        lax.all_to_all(out_rows, "query", split_axis=1, concat_axis=1, tiled=True),
        lax.all_to_all(packed_keys, "query", split_axis=1, concat_axis=1, tiled=True),
    )
    inputs_side = inputs_side[0]
    grads_side = grads_side[0]
    keys_side = keys_side[0]
    doc_of_row = keys_side // 65536
    pos_of_row = keys_side % 65536
    live_mask = (doc_of_row[:, None] == jnp.arange(doc_count, dtype=jnp.int32)[None, :]) & (
        pos_of_row[:, None] < doc_len[0][None, :]
    )
    weights = live_mask.astype(jnp.bfloat16)
    row_count = inputs_side.shape[0]
    row_span = math.gcd(row_count, 1024)

    def accumulate(turn_index, running):
        row_start = turn_index * row_span
        x_part = lax.dynamic_slice_in_dim(inputs_side, row_start, row_span, 0)
        g_part = lax.dynamic_slice_in_dim(grads_side, row_start, row_span, 0)
        w_part = lax.dynamic_slice_in_dim(weights, row_start, row_span, 0)
        spread = (w_part[:, :, None] * x_part[:, None, :]).reshape(row_span, doc_count * in_width)
        return running + lax.dot_general(
            g_part, spread, (((0,), (0,)), ((), ())), preferred_element_type=jnp.float32
        )

    gradients = jnp.zeros((grads_side.shape[1], doc_count * in_width), jnp.float32)
    gradients = lax.fori_loop(0, row_count // row_span, accumulate, gradients)
    scaling = 1.0 / (eig_out[:, None] * eig_in[None, :] + damping)
    query_block = precondition(gradients, scaling, basis_in, basis_out)
    train_slab = train_feats[0]
    store_count = lax.axis_size("store")
    own_index = lax.axis_index("store")
    score_table = jnp.zeros((store_count * doc_count, train_slab.shape[0]), jnp.bfloat16)

    def travel(carry, visit_index):
        moving, table_now = carry
        table_now = record(table_now, moving, (own_index - visit_index) % store_count, train_slab)
        moving = from_behind(moving, "store", 1)
        return ((moving, table_now), None)

    (moving, score_table), _ = lax.scan(
        travel, (query_block, score_table), jnp.arange(store_count - 1, dtype=jnp.int32)
    )
    score_table = record(
        score_table, moving, (own_index - (store_count - 1)) % store_count, train_slab
    )
    return score_table[None]


def solution(mesh):
    placed = (
        P("query", "store", None),
        P("query", "store", None),
        P("query", "store"),
        P("query", "store"),
        P("query", "store"),
        P(),
        P(),
        P(),
        P(),
        P("query", "store", None),
    )
    return jax.shard_map(
        on_device, mesh=mesh, in_specs=placed, out_specs=P("query", None, "store"), check_vma=False
    )
```

profile of v0, /device:TPU:0, one launch (start us, length us, event | category | flops | bytes accessed | tf_op | source)
XLA Modules:
  0.0 183.5 jit_solution(18066739965186172153)
XLA Ops:
  1.4 7.3 %all-to-all-start.1 = ((s32[1,8,512]{2,0,1:T(1,128)}), s32[1,8,512]{2,0,1:T(1,128)S(1)}, u32[]{:S(2)}, u32[]{:S(2)}) async-start(s32[1,8,512]{2,0,1:T(1,128)} %bitcast.1), calls=%async_computation.1 | async-start | bytes 32768 | tf_op jit(solution)/shard_map/all_to_all | solution.py:55
  8.7 4.9 %copy.27 = bf16[1,4096,64]{2,0,1:T(2,128)(2,1)S(1)} copy(bf16[1,4096,64]{1,2,0:T(8,128)(2,1)} %param.14) | data formatting | bytes 1048576 | tf_op args[0]
  14.1 22.3 %reduce.1 = bf16[4096,64]{1,0:T(8,128)(2,1)S(1)} reduce(bf16[4096,1,64]{2,1,0:T(2,128)(2,1)S(1)} %bitcast.60, bf16[]{:T(256)} %broadcast.96), dimensions={1}, to_apply=%bitcast.31.reduce_sub_computation | reduce | bytes 1048578
  37.9 6.0 %all-to-all-start.2 = ((bf16[8,2,16384]{2,1,0:T(2,128)(2,1)}), bf16[8,2,16384]{2,1,0:T(2,128)(2,1)}, u32[]{:S(2)}, u32[]{:S(2)}) async-start(bf16[8,2,16384]{2,1,0:T(2,128)(2,1)} %reshape.110), calls=%async_computation.2 | async-start | bytes 1048576 | tf_op jit(solution)/shard_map/all_to_all | solution.py:53
  43.9 3.2 %copy.39 = bf16[1,4096,128]{2,0,1:T(2,128)(2,1)S(1)} copy(bf16[1,4096,128]{2,1,0:T(8,128)(2,1)} %param.15) | data formatting | bytes 2097152 | tf_op args[1]
  47.1 22.3 %reduce = bf16[4096,128]{1,0:T(8,128)(2,1)S(1)} reduce(bf16[4096,1,128]{2,1,0:T(2,128)(2,1)S(1)} %bitcast.62, bf16[]{:T(256)} %broadcast.96), dimensions={1}, to_apply=%bitcast.45.reduce_sub_computation | reduce | bytes 2097154
  70.6 6.0 %all-to-all-start = ((bf16[8,2,32768]{2,1,0:T(2,128)(2,1)}), bf16[8,2,32768]{2,1,0:T(2,128)(2,1)}, u32[]{:S(2)}, u32[]{:S(2)}) async-start(bf16[8,2,32768]{2,1,0:T(2,128)(2,1)} %reshape.108), calls=%async_computation | async-start | bytes 2097152 | tf_op jit(solution)/shard_map/all_to_all | solution.py:54
  76.9 4.1 %reshape.111 = bf16[4096,1,64]{2,1,0:T(2,128)(2,1)S(1)} reshape(bf16[8,2,16384]{2,1,0:T(2,128)(2,1)} %all-to-all-done.2) | data formatting | bytes 1048576
  81.0 3.6 %copy.28 = bf16[1,4096,64]{1,2,0:T(8,128)(2,1)} copy(bf16[1,4096,64]{2,0,1:T(2,128)(2,1)S(1)} %bitcast.59) | data formatting | bytes 1048576 | tf_op jit(solution)/shard_map/all_to_all | solution.py:53
  84.7 16.9 %all-to-all-done = bf16[8,2,32768]{2,1,0:T(2,128)(2,1)} async-done(((bf16[8,2,32768]{2,1,0:T(2,128)(2,1)}), bf16[8,2,32768]{2,1,0:T(2,128)(2,1)}, u32[]{:S(2)}, u32[]{:S(2)}) %all-to-all-start) | async-done | bytes 1048608 | tf_op jit(solution)/shard_map/all_to_all | solution.py:54
  101.5 4.3 %reshape.109 = bf16[4096,1,128]{2,1,0:T(2,128)(2,1)S(1)} reshape(bf16[8,2,32768]{2,1,0:T(2,128)(2,1)} %all-to-all-done) | data formatting | bytes 2097152
  107.0 28.7 %while.29 = (s32[]{:T(128)}, f32[128,2048]{1,0:T(8,128)S(1)}, bf16[4096,128]{1,0:T(8,128)(2,1)}, bf16[4096,32]{0,1:T(8,128)(2,1)S(1)}, bf16[4096,64]{0,1:T(8,128...) while((s32[]{:T(128)}, f32[128,2048]{1,0:T(8,128)S(1)}, bf16[4096,128]{1,0:T(8,128)(2,1)}, ...), condition=%wide.region_1.2_spmd.clone, body=%wide.region_0.1_spmd.clone.sunk | while | flops 539492352 | bytes 11337897 | solution.py:80
  107.9 2.2 %broadcast_multiply_fusion.2 = bf16[1024,32,64]{0,2,1:T(8,128)(2,1)} fusion(bf16[1024,64]{0,1:T(8,128)(2,1)S(1)} %constant_dynamic-slice_fusion.4, bf16[1024,32]{0,1:T(8,128)(2,1)S(1)} %constant_dynamic-slice_fusion.5), kind=kLoop, calls=%fused_computation.3.clone.1 | loop fusion | flops 2097152 | bytes 4390912 | tf_op jit(solution)/shard_map/while/body/eval_jaxpr/mul | solution.py:74
  110.1 4.0 %convolution_add_fusion.2 = f32[128,2048]{1,0:T(8,128)S(1)} fusion(bf16[1024,2048]{0,1:T(8,128)(2,1)} %bitcast.56, f32[128,2048]{1,0:T(8,128)S(1)} %get-tuple-element.306, pred[]{:T(512)S(6)} %compare.16, bf16[4096,128]{1,0:T(8,128)(2,1)} %get-tuple-element.316, s32[]{:T(128)S(6)} %select_n.65), kind=kOutput, calls=%fused_computation.2.clone.1 | convolution fusion | flops 537395200 | bytes 6553605 | tf_op jit(solution)/shard_map/while/body/eval_jaxpr/dot_general | solution.py:75
  115.1 2.2 %broadcast_multiply_fusion.2 = bf16[1024,32,64]{0,2,1:T(8,128)(2,1)} fusion(bf16[1024,64]{0,1:T(8,128)(2,1)S(1)} %constant_dynamic-slice_fusion.4, bf16[1024,32]{0,1:T(8,128)(2,1)S(1)} %constant_dynamic-slice_fusion.5), kind=kLoop, calls=%fused_computation.3.clone.1 | loop fusion | flops 2097152 | bytes 4390912 | tf_op jit(solution)/shard_map/while/body/eval_jaxpr/mul | solution.py:74
  117.3 4.0 %convolution_add_fusion.2 = f32[128,2048]{1,0:T(8,128)S(1)} fusion(bf16[1024,2048]{0,1:T(8,128)(2,1)} %bitcast.56, f32[128,2048]{1,0:T(8,128)S(1)} %get-tuple-element.306, pred[]{:T(512)S(6)} %compare.16, bf16[4096,128]{1,0:T(8,128)(2,1)} %get-tuple-element.316, s32[]{:T(128)S(6)} %select_n.65), kind=kOutput, calls=%fused_computation.2.clone.1 | convolution fusion | flops 537395200 | bytes 6553605 | tf_op jit(solution)/shard_map/while/body/eval_jaxpr/dot_general | solution.py:75
  124.5 4.0 %convolution_add_fusion.2 = f32[128,2048]{1,0:T(8,128)S(1)} fusion(bf16[1024,2048]{0,1:T(8,128)(2,1)} %bitcast.56, f32[128,2048]{1,0:T(8,128)S(1)} %get-tuple-element.306, pred[]{:T(512)S(6)} %compare.16, bf16[4096,128]{1,0:T(8,128)(2,1)} %get-tuple-element.316, s32[]{:T(128)S(6)} %select_n.65), kind=kOutput, calls=%fused_computation.2.clone.1 | convolution fusion | flops 537395200 | bytes 6553605 | tf_op jit(solution)/shard_map/while/body/eval_jaxpr/dot_general | solution.py:75
  131.7 4.0 %convolution_add_fusion.2 = f32[128,2048]{1,0:T(8,128)S(1)} fusion(bf16[1024,2048]{0,1:T(8,128)(2,1)} %bitcast.56, f32[128,2048]{1,0:T(8,128)S(1)} %get-tuple-element.306, pred[]{:T(512)S(6)} %compare.16, bf16[4096,128]{1,0:T(8,128)(2,1)} %get-tuple-element.316, s32[]{:T(128)S(6)} %select_n.65), kind=kOutput, calls=%fused_computation.2.clone.1 | convolution fusion | flops 537395200 | bytes 6553605 | tf_op jit(solution)/shard_map/while/body/eval_jaxpr/dot_general | solution.py:75
  141.5 2.4 %copy.30 = bf16[32,128,64]{2,1,0:T(8,128)(2,1)} copy(bf16[32,128,64]{1,2,0:T(8,128)(2,1)} %fusion.3) | data formatting | bytes 1048576 | tf_op jit(solution)/shard_map/convert_element_type | solution.py:33
  143.9 2.7 %convert_element_type.24 = bf16[32,8192]{1,0:T(8,128)(2,1)} reshape(bf16[32,128,64]{2,1,0:T(8,128)(2,1)} %copy.30) | data formatting | bytes 1048576 | tf_op jit(solution)/shard_map/convert_element_type | solution.py:33
  146.6 32.4 %while.28 = (s32[]{:T(128)}, bf16[32,8192]{1,0:T(8,128)(2,1)}, bf16[128,192]{1,0:T(8,128)(2,1)S(1)}, bf16[192,8192]{1,0:T(8,128)(2,1)S(1)}, s32[3]{0:T(128)S(1)}...) while((s32[]{:T(128)}, bf16[32,8192]{1,0:T(8,128)(2,1)}, ...), condition=%wide.region_3.4_spmd, body=%wide.region_2.3_spmd.sunk | while | flops 100669456 | bytes 6832468 | solution.py:94
  151.8 5.6 %collective-permute-done = bf16[32,8192]{1,0:T(8,128)(2,1)} collective-permute-done((bf16[32,8192]{1,0:T(8,128)(2,1)}, bf16[32,8192]{1,0:T(8,128)(2,1)}, u32[]{:S(2)}, u32[]{:S(2)}) %collective-permute-start) | collective-permute-done | bytes 524320 | tf_op jit(solution)/shard_map/while/body/eval_jaxpr/ppermute | solution.py:13
  162.6 5.6 %collective-permute-done = bf16[32,8192]{1,0:T(8,128)(2,1)} collective-permute-done((bf16[32,8192]{1,0:T(8,128)(2,1)}, bf16[32,8192]{1,0:T(8,128)(2,1)}, u32[]{:S(2)}, u32[]{:S(2)}) %collective-permute-start) | collective-permute-done | bytes 524320 | tf_op jit(solution)/shard_map/while/body/eval_jaxpr/ppermute | solution.py:13
  173.4 5.6 %collective-permute-done = bf16[32,8192]{1,0:T(8,128)(2,1)} collective-permute-done((bf16[32,8192]{1,0:T(8,128)(2,1)}, bf16[32,8192]{1,0:T(8,128)(2,1)}, u32[]{:S(2)}, u32[]{:S(2)}) %collective-permute-start) | collective-permute-done | bytes 524320 | tf_op jit(solution)/shard_map/while/body/eval_jaxpr/ppermute | solution.py:13
  (55 shorter events, 38.1 us)
Async XLA Ops:
  0.0 135.7 %copy-start = (f32[128,128]{1,0:T(8,128)S(1)}, f32[128,128]{1,0:T(8,128)}, u32[]{:S(2)}) copy-start(f32[128,128]{1,0:T(8,128)} %param.22) | copy-start | bytes 196612
  1.4 36.5 %all-to-all-start.1 = ((s32[1,8,512]{2,0,1:T(1,128)}), s32[1,8,512]{2,0,1:T(1,128)S(1)}, u32[]{:S(2)}, u32[]{:S(2)}) async-start(s32[1,8,512]{2,0,1:T(1,128)} %bitcast.1), calls=%async_computation.1 | async-start | bytes 32768 | tf_op jit(solution)/shard_map/all_to_all | solution.py:55
  37.9 32.6 %all-to-all-start.2 = ((bf16[8,2,16384]{2,1,0:T(2,128)(2,1)}), bf16[8,2,16384]{2,1,0:T(2,128)(2,1)}, u32[]{:S(2)}, u32[]{:S(2)}) async-start(bf16[8,2,16384]{2,1,0:T(2,128)(2,1)} %reshape.110), calls=%async_computation.2 | async-start | bytes 1048576 | tf_op jit(solution)/shard_map/all_to_all | solution.py:53
  47.1 29.5 %copy-start.3 = (f32[64]{0:T(128)S(1)}, f32[64]{0:T(128)}, u32[]{:S(2)}) copy-start(f32[64]{0:T(128)} %param.19) | copy-start | bytes 772
  47.1 29.5 %copy-start.4 = (f32[128]{0:T(128)S(1)}, f32[128]{0:T(128)}, u32[]{:S(2)}) copy-start(f32[128]{0:T(128)} %param.20) | copy-start | bytes 1540
  47.1 29.6 %copy-start.5 = (s32[1,32]{1,0:T(1,128)S(1)}, s32[1,32]{1,0:T(1,128)}, u32[]{:S(2)}) copy-start(s32[1,32]{1,0:T(1,128)} %param.18) | copy-start | bytes 388
  70.6 31.0 %all-to-all-start = ((bf16[8,2,32768]{2,1,0:T(2,128)(2,1)}), bf16[8,2,32768]{2,1,0:T(2,128)(2,1)}, u32[]{:S(2)}, u32[]{:S(2)}) async-start(bf16[8,2,32768]{2,1,0:T(2,128)(2,1)} %reshape.108), calls=%async_computation | async-start | bytes 2097152 | tf_op jit(solution)/shard_map/all_to_all | solution.py:54
  107.0 30.5 %copy-start.2 = (f32[64,64]{1,0:T(8,128)S(1)}, f32[64,64]{1,0:T(8,128)}, u32[]{:S(2)}) copy-start(f32[64,64]{1,0:T(8,128)} %param.21) | copy-start | bytes 49156
  138.6 8.0 %copy-start.1 = (bf16[1,192,8192]{2,1,0:T(8,128)(2,1)S(1)}, bf16[1,192,8192]{2,1,0:T(8,128)(2,1)}, u32[]{:S(2)}) copy-start(bf16[1,192,8192]{2,1,0:T(8,128)(2,1)} %param.23) | copy-start | bytes 9437188
  148.5 8.9 %collective-permute-start = (bf16[32,8192]{1,0:T(8,128)(2,1)}, bf16[32,8192]{1,0:T(8,128)(2,1)}, u32[]{:S(2)}, u32[]{:S(2)}) collective-permute-start(bf16[32,8192]{1,0:T(8,128)(2,1)} %copy.51), channel_id=1, source_target_pairs={{0,1},{1,2},{2,3},{3,0},{4,5},{5,6},{6,7},{7,4},{8,9},{9,10},{10,1... | collective-permute-start | bytes 1572872 | tf_op jit(solution)/shard_map/while/body/eval_jaxpr/ppermute | solution.py:13
  159.3 8.9 %collective-permute-start = (bf16[32,8192]{1,0:T(8,128)(2,1)}, bf16[32,8192]{1,0:T(8,128)(2,1)}, u32[]{:S(2)}, u32[]{:S(2)}) collective-permute-start(bf16[32,8192]{1,0:T(8,128)(2,1)} %copy.51), channel_id=1, source_target_pairs={{0,1},{1,2},{2,3},{3,0},{4,5},{5,6},{6,7},{7,4},{8,9},{9,10},{10,1... | collective-permute-start | bytes 1572872 | tf_op jit(solution)/shard_map/while/body/eval_jaxpr/ppermute | solution.py:13
  170.1 8.9 %collective-permute-start = (bf16[32,8192]{1,0:T(8,128)(2,1)}, bf16[32,8192]{1,0:T(8,128)(2,1)}, u32[]{:S(2)}, u32[]{:S(2)}) collective-permute-start(bf16[32,8192]{1,0:T(8,128)(2,1)} %copy.51), channel_id=1, source_target_pairs={{0,1},{1,2},{2,3},{3,0},{4,5},{5,6},{6,7},{7,4},{8,9},{9,10},{10,1... | collective-permute-start | bytes 1572872 | tf_op jit(solution)/shard_map/while/body/eval_jaxpr/ppermute | solution.py:13
where the time goes:
time: 185 us; the launch traced here: 184 us
  other arithmetic  55.2 us (30%)
  local copies, waits for them, and re-layouts  43 us (23%)
  waiting for transfers between devices  33.7 us (18%)
  matrix products  30.1 us (16%)
  starting transfers between devices  19.3 us (10%)
  loops' own time  1.96 us (1%)
    unnamed x3, other arithmetic  44.6 us
    unnamed x20, local copies, waits for them, and re-layouts  20.8 us
    all_to_all x1, waiting for transfers between devices, on_device(): lax.all_to_all(out_rows, 'query', split_axis=1, concat_axis=1, tiled=True)  16.9 us
    ppermute x3, waiting for transfers between devices, from_behind(): lax.ppermute(x, axis, [(i, (i + by) % devices) for i in range(devices)])  16.9 us
    dot_general x4, matrix products, accumulate(): lax.dot_general(g_part, spread, (((0,), (0,)), ((), ())), preferred_eleme...  15.9 us
    mul x4, other arithmetic, accumulate(): w_part[:, :, None] * x_part[:, None, :]  8.93 us
    dot_general x4, matrix products, record(): lax.dot_general(query_block, train_slab, (((1,), (1,)), ((), ())), prefer...  8.42 us
    all_to_all x1, starting transfers between devices, on_device(): lax.all_to_all(packed_keys, 'query', split_axis=1, concat_axis=1, tiled=T...  7.31 us
  transfers between devices with their start and end apart: 6, of which 4 were waited for; matrix products, arithmetic and copies ran while one was open for 39% of the time, Pallas kernels for 0%

commit v1 on v0

--- a/solution.py
+++ b/solution.py
@@ -6,6 +6,22 @@
 
 damping = 0.1
 highest = lax.Precision.HIGHEST
+
+
+def pairwise_exchange(array, axis, split, join):
+    ways, here = (lax.axis_size(axis), lax.axis_index(axis))
+    width = array.shape[split] // ways
+    shape = list(array.shape)
+    shape[split] = width
+    height = shape[join]
+    shape[join] = height * ways
+    full = jnp.zeros(shape, array.dtype)
+    for mask in range(ways):
+        part = lax.dynamic_slice_in_dim(array, (here ^ mask) * width, width, axis=split)
+        if mask:
+            part = lax.ppermute(part, axis, [(d, d ^ mask) for d in range(ways)])
+        full = lax.dynamic_update_slice_in_dim(full, part, (here ^ mask) * height, axis=join)
+    return full
 
 
 def from_behind(x, axis, by):
@@ -50,7 +66,7 @@
     in_width = in_rows.shape[2]
     packed_keys = row_doc * 65536 + row_pos
     inputs_side, grads_side, keys_side = (
-        lax.all_to_all(in_rows, "query", split_axis=1, concat_axis=1, tiled=True),
+        pairwise_exchange(in_rows, "query", 1, 1),
         lax.all_to_all(out_rows, "query", split_axis=1, concat_axis=1, tiled=True),
         lax.all_to_all(packed_keys, "query", split_axis=1, concat_axis=1, tiled=True),
     )

time: 185 us -> 170 us (0.919)
  other arithmetic: 55.2 us -> 34.5 us
  starting transfers between devices: 19.3 us -> 25.1 us
    unnamed x3 -> x2, other arithmetic: 44.6 us -> 23.3 us
    ppermute x0 -> x7, waiting for transfers between devices: none -> 18.1 us  [pairwise_exchange(): part = lax.ppermute(part, axis, [(d, d ^ mask) for d in range(ways)])]
    all_to_all x1, waiting for transfers between devices: 16.9 us -> 0.01 us  [on_device(): lax.all_to_all(out_rows, 'query', split_axis=1, concat_axis=1, tiled=True)]
    ppermute x0 -> x7, starting transfers between devices: none -> 15.3 us  [pairwise_exchange(): part = lax.ppermute(part, axis, [(d, d ^ mask) for d in range(ways)])]
    unnamed x20 -> x19, local copies, waits for them, and re-layouts: 20.8 us -> 11.3 us
    dynamic_update_slice x0 -> x8, local copies, waits for them, and re-layouts: none -> 9.33 us  [pairwise_exchange(): lax.dynamic_update_slice_in_dim(full, part, (here ^ mask) * height, axis=...]
    all_to_all x1 -> x0, starting transfers between devices: 5.99 us -> none  [on_device(): lax.all_to_all(in_rows, 'query', split_axis=1, concat_axis=1, tiled=True)]
    all_to_all x1 -> x0, local copies, waits for them, and re-layouts: 3.63 us -> none  [on_device(): lax.all_to_all(in_rows, 'query', split_axis=1, concat_axis=1, tiled=True)]
  transfers between devices with their start and end apart: 6 -> 12, of which waited for: 4 -> 4; matrix products, arithmetic and copies ran while one was open for 39% -> 29% of each run, Pallas kernels for 0% -> 0%
where the time goes in v1:
time: 170 us; the launch traced here: 169 us
  local copies, waits for them, and re-layouts  42 us (25%)
  waiting for transfers between devices  34.8 us (20%)
  other arithmetic  34.5 us (20%)
  matrix products  30.1 us (18%)
  starting transfers between devices  25.1 us (15%)
  loops' own time  2.17 us (1%)
    unnamed x2, other arithmetic  23.3 us
    ppermute x7, waiting for transfers between devices, pairwise_exchange(): part = lax.ppermute(part, axis, [(d, d ^ mask) for d in range(ways)])  18.1 us
    ppermute x3, waiting for transfers between devices, from_behind(): lax.ppermute(x, axis, [(i, (i + by) % devices) for i in range(devices)])  16.7 us
    dot_general x4, matrix products, accumulate(): lax.dot_general(g_part, spread, (((0,), (0,)), ((), ())), preferred_eleme...  15.9 us
    ppermute x7, starting transfers between devices, pairwise_exchange(): part = lax.ppermute(part, axis, [(d, d ^ mask) for d in range(ways)])  15.3 us
    unnamed x19, local copies, waits for them, and re-layouts  11.3 us
    dynamic_update_slice x8, local copies, waits for them, and re-layouts, pairwise_exchange(): lax.dynamic_update_slice_in_dim(full, part, (here ^ mask) * height, axis=...  9.33 us
    mul x4, other arithmetic, accumulate(): w_part[:, :, None] * x_part[:, None, :]  8.93 us
  transfers between devices with their start and end apart: 12, of which 4 were waited for; matrix products, arithmetic and copies ran while one was open for 29% of the time, Pallas kernels for 0%

profile of v1, /device:TPU:0, one launch (start us, length us, event | category | flops | bytes accessed | tf_op | source)
XLA Modules:
  0.0 168.8 jit_solution(12254332946562195647)
XLA Ops:
  1.9 3.0 %collective-permute-start.1 = (bf16[1,512,64]{1,2,0:T(8,128)(2,1)}, bf16[1,512,64]{1,2,0:T(8,128)(2,1)}, u32[]{:S(2)}, u32[]{:S(2)}) collective-permute-start(bf16[1,512,64]{1,2,0:T(8,128)(2,1)} %get-tuple-element.226), channel_id=1, source_target_pairs={{0,4},{4,0},{8,12},{12,8},{16,20},{20,16},{24,28},{28,24},{1,5},{5... | collective-permute-start | bytes 196616 | tf_op jit(solution)/shard_map/ppermute | solution.py:22
  6.4 3.0 %collective-permute-start.4 = (bf16[1,512,64]{1,2,0:T(8,128)(2,1)}, bf16[1,512,64]{1,2,0:T(8,128)(2,1)}, u32[]{:S(2)}, u32[]{:S(2)}) collective-permute-start(bf16[1,512,64]{1,2,0:T(8,128)(2,1)} %get-tuple-element.223), channel_id=1, source_target_pairs={{0,16},{4,20},{8,24},{12,28},{16,0},{20,4},{24,8},{28,12},{1,17},{... | collective-permute-start | bytes 196616 | tf_op jit(solution)/shard_map/ppermute | solution.py:22
  10.8 3.8 %all-to-all-start.1 = ((s32[1,8,512]{2,0,1:T(1,128)}), s32[1,8,512]{2,0,1:T(1,128)S(1)}, u32[]{:S(2)}, u32[]{:S(2)}) async-start(s32[1,8,512]{2,0,1:T(1,128)} %bitcast.1), calls=%async_computation.1 | async-start | bytes 32768 | tf_op jit(solution)/shard_map/all_to_all | solution.py:71
  17.7 3.2 %copy.42 = bf16[1,4096,128]{2,0,1:T(2,128)(2,1)S(1)} copy(bf16[1,4096,128]{2,1,0:T(8,128)(2,1)} %param.15) | data formatting | bytes 2097152 | tf_op args[1]
  21.4 23.3 %reduce = bf16[4096,128]{1,0:T(8,128)(2,1)} reduce(bf16[4096,1,128]{2,1,0:T(2,128)(2,1)S(1)} %bitcast.73, bf16[]{:T(256)} %broadcast.102), dimensions={1}, to_apply=%bitcast.58.reduce_sub_computation | reduce | bytes 2097154
  46.9 6.0 %all-to-all-start = ((bf16[8,2,32768]{2,1,0:T(2,128)(2,1)}), bf16[8,2,32768]{2,1,0:T(2,128)(2,1)}, u32[]{:S(2)}, u32[]{:S(2)}) async-start(bf16[8,2,32768]{2,1,0:T(2,128)(2,1)} %reshape.124), calls=%async_computation | async-start | bytes 2097152 | tf_op jit(solution)/shard_map/all_to_all | solution.py:70
  53.1 3.9 %collective-permute-start.5 = (bf16[1,512,64]{1,2,0:T(8,128)(2,1)S(1)}, bf16[1,512,64]{1,2,0:T(8,128)(2,1)S(1)}, u32[]{:S(2)}, u32[]{:S(2)}) collective-permute-start(bf16[1,512,64]{1,2,0:T(8,128)(2,1)S(1)} %copy-done.5), channel_id=1, source_target_pairs={{0,20},{4,16},{8,28},{12,24},{16,4},{20,0},{24,12},{28,8},{1,21},{... | collective-permute-start | bytes 196616 | tf_op jit(solution)/shard_map/ppermute | solution.py:22
  61.4 2.4 %collective-permute-start.7 = (bf16[1,512,64]{1,2,0:T(8,128)(2,1)S(1)}, bf16[1,512,64]{1,2,0:T(8,128)(2,1)S(1)}, u32[]{:S(2)}, u32[]{:S(2)}) collective-permute-start(bf16[1,512,64]{1,2,0:T(8,128)(2,1)S(1)} %copy-done.3), channel_id=1, source_target_pairs={{0,28},{4,24},{8,20},{12,16},{16,12},{20,8},{24,4},{28,0},{1,29},{... | collective-permute-start | bytes 196616 | tf_op jit(solution)/shard_map/ppermute | solution.py:22
  66.7 18.1 %collective-permute-done.5 = bf16[1,512,64]{1,2,0:T(8,128)(2,1)S(1)} collective-permute-done((bf16[1,512,64]{1,2,0:T(8,128)(2,1)S(1)}, bf16[1,512,64]{1,2,0:T(8,128)(2,1)S(1)}, u32[]{:S(2)}, u32[]{:S(2)}) %collective-permute-start.5) | collective-permute-done | bytes 65568 | tf_op jit(solution)/shard_map/ppermute | solution.py:22
  86.8 4.3 %reshape.125 = bf16[4096,1,128]{2,1,0:T(2,128)(2,1)S(1)} reshape(bf16[8,2,32768]{2,1,0:T(2,128)(2,1)} %all-to-all-done) | data formatting | bytes 2097152
  92.2 28.7 %while.29 = (s32[]{:T(128)}, f32[128,2048]{1,0:T(8,128)S(1)}, bf16[4096,128]{1,0:T(8,128)(2,1)}, bf16[4096,32]{0,1:T(8,128)(2,1)S(1)}, bf16[4096,64]{0,1:T(8,128...) while((s32[]{:T(128)}, f32[128,2048]{1,0:T(8,128)S(1)}, bf16[4096,128]{1,0:T(8,128)(2,1)}, ...), condition=%wide.region_1.2_spmd.clone, body=%wide.region_0.1_spmd.clone.sunk | while | flops 539492352 | bytes 11337889 | solution.py:96
  93.1 2.2 %broadcast_multiply_fusion.2 = bf16[1024,32,64]{0,2,1:T(8,128)(2,1)} fusion(bf16[1024,64]{0,1:T(8,128)(2,1)S(1)} %constant_dynamic-slice_fusion.11, bf16[1024,32]{0,1:T(8,128)(2,1)S(1)} %constant_dynamic-slice_fusion.12), kind=kLoop, calls=%fused_computation.3.clone.1 | loop fusion | flops 2097152 | bytes 4390912 | tf_op jit(solution)/shard_map/while/body/eval_jaxpr/mul | solution.py:90
  95.4 4.0 %convolution_add_fusion.2 = f32[128,2048]{1,0:T(8,128)S(1)} fusion(bf16[1024,2048]{0,1:T(8,128)(2,1)} %bitcast.69, f32[128,2048]{1,0:T(8,128)S(1)} %get-tuple-element.308, pred[]{:T(512)S(6)} %compare.16, bf16[4096,128]{1,0:T(8,128)(2,1)} %get-tuple-element.318, s32[]{:T(128)S(6)} %select_n.105), kind=kOutput, calls=%fused_computation.2.clone.1 | convolution fusion | flops 537395200 | bytes 6553605 | tf_op jit(solution)/shard_map/while/body/eval_jaxpr/dot_general | solution.py:91
  100.3 2.2 %broadcast_multiply_fusion.2 = bf16[1024,32,64]{0,2,1:T(8,128)(2,1)} fusion(bf16[1024,64]{0,1:T(8,128)(2,1)S(1)} %constant_dynamic-slice_fusion.11, bf16[1024,32]{0,1:T(8,128)(2,1)S(1)} %constant_dynamic-slice_fusion.12), kind=kLoop, calls=%fused_computation.3.clone.1 | loop fusion | flops 2097152 | bytes 4390912 | tf_op jit(solution)/shard_map/while/body/eval_jaxpr/mul | solution.py:90
  102.6 4.0 %convolution_add_fusion.2 = f32[128,2048]{1,0:T(8,128)S(1)} fusion(bf16[1024,2048]{0,1:T(8,128)(2,1)} %bitcast.69, f32[128,2048]{1,0:T(8,128)S(1)} %get-tuple-element.308, pred[]{:T(512)S(6)} %compare.16, bf16[4096,128]{1,0:T(8,128)(2,1)} %get-tuple-element.318, s32[]{:T(128)S(6)} %select_n.105), kind=kOutput, calls=%fused_computation.2.clone.1 | convolution fusion | flops 537395200 | bytes 6553605 | tf_op jit(solution)/shard_map/while/body/eval_jaxpr/dot_general | solution.py:91
  107.5 2.2 %broadcast_multiply_fusion.2 = bf16[1024,32,64]{0,2,1:T(8,128)(2,1)} fusion(bf16[1024,64]{0,1:T(8,128)(2,1)S(1)} %constant_dynamic-slice_fusion.11, bf16[1024,32]{0,1:T(8,128)(2,1)S(1)} %constant_dynamic-slice_fusion.12), kind=kLoop, calls=%fused_computation.3.clone.1 | loop fusion | flops 2097152 | bytes 4390912 | tf_op jit(solution)/shard_map/while/body/eval_jaxpr/mul | solution.py:90
  109.7 4.0 %convolution_add_fusion.2 = f32[128,2048]{1,0:T(8,128)S(1)} fusion(bf16[1024,2048]{0,1:T(8,128)(2,1)} %bitcast.69, f32[128,2048]{1,0:T(8,128)S(1)} %get-tuple-element.308, pred[]{:T(512)S(6)} %compare.16, bf16[4096,128]{1,0:T(8,128)(2,1)} %get-tuple-element.318, s32[]{:T(128)S(6)} %select_n.105), kind=kOutput, calls=%fused_computation.2.clone.1 | convolution fusion | flops 537395200 | bytes 6553605 | tf_op jit(solution)/shard_map/while/body/eval_jaxpr/dot_general | solution.py:91
  116.9 4.0 %convolution_add_fusion.2 = f32[128,2048]{1,0:T(8,128)S(1)} fusion(bf16[1024,2048]{0,1:T(8,128)(2,1)} %bitcast.69, f32[128,2048]{1,0:T(8,128)S(1)} %get-tuple-element.308, pred[]{:T(512)S(6)} %compare.16, bf16[4096,128]{1,0:T(8,128)(2,1)} %get-tuple-element.318, s32[]{:T(128)S(6)} %select_n.105), kind=kOutput, calls=%fused_computation.2.clone.1 | convolution fusion | flops 537395200 | bytes 6553605 | tf_op jit(solution)/shard_map/while/body/eval_jaxpr/dot_general | solution.py:91
  126.7 2.4 %copy.33 = bf16[32,128,64]{2,1,0:T(8,128)(2,1)} copy(bf16[32,128,64]{1,2,0:T(8,128)(2,1)} %fusion.3) | data formatting | bytes 1048576 | tf_op jit(solution)/shard_map/convert_element_type | solution.py:49
  129.1 2.7 %convert_element_type.24 = bf16[32,8192]{1,0:T(8,128)(2,1)} reshape(bf16[32,128,64]{2,1,0:T(8,128)(2,1)} %copy.33) | data formatting | bytes 1048576 | tf_op jit(solution)/shard_map/convert_element_type | solution.py:49
  131.8 32.4 %while.28 = (s32[]{:T(128)}, bf16[32,8192]{1,0:T(8,128)(2,1)}, bf16[128,192]{1,0:T(8,128)(2,1)S(1)}, bf16[192,8192]{1,0:T(8,128)(2,1)S(1)}, s32[3]{0:T(128)S(1)}...) while((s32[]{:T(128)}, bf16[32,8192]{1,0:T(8,128)(2,1)}, ...), condition=%wide.region_3.4_spmd, body=%wide.region_2.3_spmd.sunk | while | flops 100669456 | bytes 6832468 | solution.py:110
  137.1 5.6 %collective-permute-done = bf16[32,8192]{1,0:T(8,128)(2,1)} collective-permute-done((bf16[32,8192]{1,0:T(8,128)(2,1)}, bf16[32,8192]{1,0:T(8,128)(2,1)}, u32[]{:S(2)}, u32[]{:S(2)}) %collective-permute-start) | collective-permute-done | bytes 524320 | tf_op jit(solution)/shard_map/while/body/eval_jaxpr/ppermute | solution.py:29
  147.9 5.6 %collective-permute-done = bf16[32,8192]{1,0:T(8,128)(2,1)} collective-permute-done((bf16[32,8192]{1,0:T(8,128)(2,1)}, bf16[32,8192]{1,0:T(8,128)(2,1)}, u32[]{:S(2)}, u32[]{:S(2)}) %collective-permute-start) | collective-permute-done | bytes 524320 | tf_op jit(solution)/shard_map/while/body/eval_jaxpr/ppermute | solution.py:29
  158.6 5.6 %collective-permute-done = bf16[32,8192]{1,0:T(8,128)(2,1)} collective-permute-done((bf16[32,8192]{1,0:T(8,128)(2,1)}, bf16[32,8192]{1,0:T(8,128)(2,1)}, u32[]{:S(2)}, u32[]{:S(2)}) %collective-permute-start) | collective-permute-done | bytes 524320 | tf_op jit(solution)/shard_map/while/body/eval_jaxpr/ppermute | solution.py:29
  (74 shorter events, 51.1 us)
Async XLA Ops:
  0.0 120.9 %copy-start = (f32[128,128]{1,0:T(8,128)S(1)}, f32[128,128]{1,0:T(8,128)}, u32[]{:S(2)}) copy-start(f32[128,128]{1,0:T(8,128)} %param.22) | copy-start | bytes 196612
  1.9 55.1 %collective-permute-start.1 = (bf16[1,512,64]{1,2,0:T(8,128)(2,1)}, bf16[1,512,64]{1,2,0:T(8,128)(2,1)}, u32[]{:S(2)}, u32[]{:S(2)}) collective-permute-start(bf16[1,512,64]{1,2,0:T(8,128)(2,1)} %get-tuple-element.226), channel_id=1, source_target_pairs={{0,4},{4,0},{8,12},{12,8},{16,20},{20,16},{24,28},{28,24},{1,5},{5... | collective-permute-start | bytes 196616 | tf_op jit(solution)/shard_map/ppermute | solution.py:22
  4.9 55.0 %collective-permute-start.2 = (bf16[1,512,64]{1,2,0:T(8,128)(2,1)}, bf16[1,512,64]{1,2,0:T(8,128)(2,1)}, u32[]{:S(2)}, u32[]{:S(2)}) collective-permute-start(bf16[1,512,64]{1,2,0:T(8,128)(2,1)} %get-tuple-element.225), channel_id=1, source_target_pairs={{0,8},{4,12},{8,0},{12,4},{16,24},{20,28},{24,16},{28,20},{1,9},{5... | collective-permute-start | bytes 196616 | tf_op jit(solution)/shard_map/ppermute | solution.py:22
  6.4 57.3 %collective-permute-start.3 = (bf16[1,512,64]{1,2,0:T(8,128)(2,1)}, bf16[1,512,64]{1,2,0:T(8,128)(2,1)}, u32[]{:S(2)}, u32[]{:S(2)}) collective-permute-start(bf16[1,512,64]{1,2,0:T(8,128)(2,1)} %get-tuple-element.224), channel_id=1, source_target_pairs={{0,12},{4,8},{8,4},{12,0},{16,28},{20,24},{24,20},{28,16},{1,13},{... | collective-permute-start | bytes 196616 | tf_op jit(solution)/shard_map/ppermute | solution.py:22
  6.4 58.8 %collective-permute-start.4 = (bf16[1,512,64]{1,2,0:T(8,128)(2,1)}, bf16[1,512,64]{1,2,0:T(8,128)(2,1)}, u32[]{:S(2)}, u32[]{:S(2)}) collective-permute-start(bf16[1,512,64]{1,2,0:T(8,128)(2,1)} %get-tuple-element.223), channel_id=1, source_target_pairs={{0,16},{4,20},{8,24},{12,28},{16,0},{20,4},{24,8},{28,12},{1,17},{... | collective-permute-start | bytes 196616 | tf_op jit(solution)/shard_map/ppermute | solution.py:22
  10.8 36.1 %all-to-all-start.1 = ((s32[1,8,512]{2,0,1:T(1,128)}), s32[1,8,512]{2,0,1:T(1,128)S(1)}, u32[]{:S(2)}, u32[]{:S(2)}) async-start(s32[1,8,512]{2,0,1:T(1,128)} %bitcast.1), calls=%async_computation.1 | async-start | bytes 32768 | tf_op jit(solution)/shard_map/all_to_all | solution.py:71
  21.4 31.5 %copy-start.6 = (s32[1,32]{1,0:T(1,128)S(1)}, s32[1,32]{1,0:T(1,128)}, u32[]{:S(2)}) copy-start(s32[1,32]{1,0:T(1,128)} %param.18) | copy-start | bytes 388
  44.7 8.4 %copy-start.5 = (bf16[1,512,64]{1,2,0:T(8,128)(2,1)S(1)}, bf16[1,512,64]{1,2,0:T(8,128)(2,1)}, u32[]{:S(2)}) copy-start(bf16[1,512,64]{1,2,0:T(8,128)(2,1)} %get-tuple-element.222) | copy-start | bytes 196612
  44.7 13.8 %copy-start.4 = (bf16[1,512,64]{1,2,0:T(8,128)(2,1)S(1)}, bf16[1,512,64]{1,2,0:T(8,128)(2,1)}, u32[]{:S(2)}) copy-start(bf16[1,512,64]{1,2,0:T(8,128)(2,1)} %get-tuple-element.227) | copy-start | bytes 196612
  44.7 16.7 %copy-start.3 = (bf16[1,512,64]{1,2,0:T(8,128)(2,1)S(1)}, bf16[1,512,64]{1,2,0:T(8,128)(2,1)}, u32[]{:S(2)}) copy-start(bf16[1,512,64]{1,2,0:T(8,128)(2,1)} %get-tuple-element.221) | copy-start | bytes 196612
  46.9 39.9 %all-to-all-start = ((bf16[8,2,32768]{2,1,0:T(2,128)(2,1)}), bf16[8,2,32768]{2,1,0:T(2,128)(2,1)}, u32[]{:S(2)}, u32[]{:S(2)}) async-start(bf16[8,2,32768]{2,1,0:T(2,128)(2,1)} %reshape.124), calls=%async_computation | async-start | bytes 2097152 | tf_op jit(solution)/shard_map/all_to_all | solution.py:70
  53.1 31.8 %collective-permute-start.5 = (bf16[1,512,64]{1,2,0:T(8,128)(2,1)S(1)}, bf16[1,512,64]{1,2,0:T(8,128)(2,1)S(1)}, u32[]{:S(2)}, u32[]{:S(2)}) collective-permute-start(bf16[1,512,64]{1,2,0:T(8,128)(2,1)S(1)} %copy-done.5), channel_id=1, source_target_pairs={{0,20},{4,16},{8,28},{12,24},{16,4},{20,0},{24,12},{28,8},{1,21},{... | collective-permute-start | bytes 196616 | tf_op jit(solution)/shard_map/ppermute | solution.py:22
  58.5 27.0 %collective-permute-start.6 = (bf16[1,512,64]{1,2,0:T(8,128)(2,1)S(1)}, bf16[1,512,64]{1,2,0:T(8,128)(2,1)S(1)}, u32[]{:S(2)}, u32[]{:S(2)}) collective-permute-start(bf16[1,512,64]{1,2,0:T(8,128)(2,1)S(1)} %copy-done.4), channel_id=1, source_target_pairs={{0,24},{4,28},{8,16},{12,20},{16,8},{20,12},{24,0},{28,4},{1,25},{... | collective-permute-start | bytes 196616 | tf_op jit(solution)/shard_map/ppermute | solution.py:22
  61.4 24.8 %collective-permute-start.7 = (bf16[1,512,64]{1,2,0:T(8,128)(2,1)S(1)}, bf16[1,512,64]{1,2,0:T(8,128)(2,1)S(1)}, u32[]{:S(2)}, u32[]{:S(2)}) collective-permute-start(bf16[1,512,64]{1,2,0:T(8,128)(2,1)S(1)} %copy-done.3), channel_id=1, source_target_pairs={{0,28},{4,24},{8,20},{12,16},{16,12},{20,8},{24,4},{28,0},{1,29},{... | collective-permute-start | bytes 196616 | tf_op jit(solution)/shard_map/ppermute | solution.py:22
  92.2 30.5 %copy-start.2 = (f32[64,64]{1,0:T(8,128)S(1)}, f32[64,64]{1,0:T(8,128)}, u32[]{:S(2)}) copy-start(f32[64,64]{1,0:T(8,128)} %param.21) | copy-start | bytes 49156
  123.8 8.0 %copy-start.1 = (bf16[1,192,8192]{2,1,0:T(8,128)(2,1)S(1)}, bf16[1,192,8192]{2,1,0:T(8,128)(2,1)}, u32[]{:S(2)}) copy-start(bf16[1,192,8192]{2,1,0:T(8,128)(2,1)} %param.23) | copy-start | bytes 9437188
  133.7 8.9 %collective-permute-start = (bf16[32,8192]{1,0:T(8,128)(2,1)}, bf16[32,8192]{1,0:T(8,128)(2,1)}, u32[]{:S(2)}, u32[]{:S(2)}) collective-permute-start(bf16[32,8192]{1,0:T(8,128)(2,1)} %copy.62), channel_id=1, source_target_pairs={{0,1},{1,2},{2,3},{3,0},{4,5},{5,6},{6,7},{7,4},{8,9},{9,10},{10,1... | collective-permute-start | bytes 1572872 | tf_op jit(solution)/shard_map/while/body/eval_jaxpr/ppermute | solution.py:29
  144.5 8.9 %collective-permute-start = (bf16[32,8192]{1,0:T(8,128)(2,1)}, bf16[32,8192]{1,0:T(8,128)(2,1)}, u32[]{:S(2)}, u32[]{:S(2)}) collective-permute-start(bf16[32,8192]{1,0:T(8,128)(2,1)} %copy.62), channel_id=1, source_target_pairs={{0,1},{1,2},{2,3},{3,0},{4,5},{5,6},{6,7},{7,4},{8,9},{9,10},{10,1... | collective-permute-start | bytes 1572872 | tf_op jit(solution)/shard_map/while/body/eval_jaxpr/ppermute | solution.py:29
  155.3 8.9 %collective-permute-start = (bf16[32,8192]{1,0:T(8,128)(2,1)}, bf16[32,8192]{1,0:T(8,128)(2,1)}, u32[]{:S(2)}, u32[]{:S(2)}) collective-permute-start(bf16[32,8192]{1,0:T(8,128)(2,1)} %copy.62), channel_id=1, source_target_pairs={{0,1},{1,2},{2,3},{3,0},{4,5},{5,6},{6,7},{7,4},{8,9},{9,10},{10,1... | collective-permute-start | bytes 1572872 | tf_op jit(solution)/shard_map/while/body/eval_jaxpr/ppermute | solution.py:29
